TPU v7x, 512 devices: a whole 4x8x8 slice. The times are simulated.
512 devices in a mesh: band: 32 (over z_lo, y), member: 16 (over x, z_hi, core).
Axes of the slice: x: 4, y: 8, z: 8 (z_hi: 2, z_lo: 4; z = z_hi * 4 + z_lo), core: 2. Of those that a mesh axis runs over, the one named last changes fastest.
Arguments:
- targets: float32 [512, 64, 4096], P(('band', 'member')), may hold values from -6 to 6
- sources: float32 [64, 64, 4096], P('band', 'member'), may hold values from -6 to 6
Outputs:
- exchange: float32 [512, 64, 4096], P(('band', 'member'))
All inputs are finite; a program needn't handle non-finite values.
Results may differ from a plain program's by a relative error of at most 0.0003.
Values sent between devices are 32-bit elements; how exact they have to be, the bound alone decides.
A program may use at most 64 MiB of HBM per device.

v0:
```python
import numpy as np
import jax
import jax.numpy as jnp
from jax import lax
from jax.experimental import pallas as pl
from jax.experimental.pallas import tpu as pltpu
from jax.sharding import PartitionSpec as P

bf16 = jnp.bfloat16
f32 = jnp.float32
MESH = pl.DeviceIdType.MESH
UNITS = 4


def split_table(table):
    high = np.asarray(table, np.float32).astype(bf16)
    low = (table - high.astype(np.float64)).astype(np.float32).astype(bf16)
    return high, low


def tables():
    wave = np.arange(64) + 1.0
    sine = np.sin(np.pi * np.outer(wave, wave) / 65)
    single = 4 * np.sin(np.pi * wave / 130) ** 2
    high, low = split_table(np.kron(np.eye(2), sine))
    right = np.block([[high, low], [high, low]])
    plane = np.broadcast_to(np.arange(64).reshape(16, 1, 4), (16, 2, 4)).reshape(-1)
    block = np.broadcast_to(np.arange(2).reshape(1, 2, 1), (16, 2, 4)).reshape(-1)
    out_wave, out_block = np.tile(np.arange(64), 2), np.repeat(np.arange(2), 64)
    left = sine[out_wave][:, plane] * (out_block[:, None] == block[None, :])
    high, low = split_table(left)
    forward = np.block([[high, high], [low, low]])
    high, low = split_table(left.T)
    backward = np.block([[high, high], [low, low]])
    middle = []
    for parity in range(2):
        one = np.kron(sine[parity::2, :32], np.eye(8))
        for matrix in (one, one.T):
            high, low = split_table(matrix)
            middle.append(np.concatenate([high, low], axis=1))
    middle = np.stack(middle).reshape(2, 2, 256, 512)
    sizes = (2, 2, 32, 8, 2, 2, 64)
    par, pair, m, s, bit, top, k3 = np.meshgrid(*[np.arange(n) for n in sizes], indexing="ij")
    k1, k2 = 32 * top + 8 * (2 * pair + bit) + s, 2 * m + par
    inverse = (2.0 / 65) ** 3 / (single[k1] + single[k2] + single[k3])
    return right, forward, backward, middle, inverse.reshape(2, 2, 256, 256).astype(np.float32)


def split(x):
    high = x.astype(bf16)
    return high, (x - high.astype(f32)).astype(bf16)


def dot(a, b):
    return jnp.dot(a, b, preferred_element_type=f32)


def exchange(a, b, low):
    return jnp.where(low, a, pltpu.roll(b, 64, 1)), jnp.where(low, pltpu.roll(a, 64, 1), b)


def forward_block(u, t, s, right, forward, wide):
    low = lax.broadcasted_iota(jnp.int32, (32, 128), 1) < 64
    d = jnp.concatenate([(t[:, v] * s[:, v]).reshape(128, 128) for v in (u, 15 - u)], axis=0)
    dh, dl = split(d)
    y = dot(jnp.concatenate([dh, dl], axis=1), right[...])
    y = y[:, :128] + y[:, 128:]
    w = [jnp.concatenate([q[:128], q[128:]], axis=1) for q in split(y)]
    z = dot(forward[...], jnp.concatenate(w, axis=0))
    z = z[:128] + z[128:]
    x = {}
    for side in range(2):
        lanes = slice(128 * side, 128 * side + 128)
        for l in range(2):
            a, b = z[64 * l : 64 * l + 32, lanes], z[64 * l + 32 : 64 * l + 64, lanes]
            x[side, l, 0], x[side, l, 1] = exchange(a, b, low)
    pairs = [(x[0, l, i], x[1, 1 - l, 1 - i]) for l in range(2) for i in range(2)]
    start = pl.multiple_of(u * 32, 32)
    for parity, parts in ((0, [a + b for a, b in pairs]), (1, [a - b for a, b in pairs])):
        for g in range(4):
            lanes = slice(128 * (g % 2), 128 * (g % 2) + 128)
            high, rest = split(jnp.concatenate([q[8 * g : 8 * g + 8] for q in parts], axis=0))
            wide[parity, g // 2, pl.ds(start, 32), lanes] = high
            wide[parity, g // 2, pl.ds(256 + start, 32), lanes] = rest


def middle_block(parity, pair, wide, middle, inverse, back):
    def times(way, high, low):
        w = middle[parity, way]
        sides = jnp.concatenate([w[:, :256], w], axis=1)
        return dot(sides, jnp.concatenate([high, low, high], axis=0))

    e = wide[parity, pair]
    q = times(0, e[:256], e[256:]) * inverse[parity, pair]
    back[parity, pair] = times(1, *split(q))


def backward_block(u, s, back, right, backward, out, first):
    low = lax.broadcasted_iota(jnp.int32, (32, 128), 1) < 64
    start = pl.multiple_of(u * 32, 32)
    total, differ = [[] for _ in range(4)], [[] for _ in range(4)]
    for g in range(4):
        lanes = slice(128 * (g % 2), 128 * (g % 2) + 128)
        even, odd = (back[p, g // 2, pl.ds(start, 32), lanes] for p in range(2))
        plus, minus = even + odd, even - odd
        for a in range(4):
            total[a].append(plus[8 * a : 8 * a + 8])
            differ[a].append(minus[8 * a : 8 * a + 8])
    total = [jnp.concatenate(q, axis=0) for q in total]
    differ = [jnp.concatenate(q, axis=0) for q in differ][::-1]
    z = []
    for side in (total, differ):
        z.append(jnp.concatenate([*exchange(side[0], side[1], low), *exchange(side[2], side[3], low)], axis=0))
    y = dot(backward[...], jnp.concatenate(split(jnp.concatenate(z, axis=1)), axis=0))
    y = y[:128] + y[128:]
    y = jnp.concatenate([y[:, :128], y[:, 128:]], axis=0)
    q = dot(jnp.concatenate(split(y), axis=1), right[...])
    q = q[:, :128] + q[:, 128:]
    for side, v in ((0, u), (1, 15 - u)):
        term = s[:, v] * q[128 * side : 128 * side + 128].reshape(16, 8, 128)
        out[:, v] = -term if first else out[:, v] - term


def swap_in(src, dst):
    top = lax.broadcasted_iota(jnp.int32, (8, 128), 0) < 4

    def step(v, carry):
        for i in range(8):
            a, b = src[2 * v, 8 * i : 8 * i + 8], src[2 * v + 1, 8 * i : 8 * i + 8]
            dst[2 * i, v] = jnp.where(top, a, pltpu.roll(b, 4, 0))
            dst[2 * i + 1, v] = jnp.where(top, pltpu.roll(a, 4, 0), b)
        return carry

    lax.fori_loop(0, 16, step, 0)


def swap_out(src, dst):
    top = lax.broadcasted_iota(jnp.int32, (8, 128), 0) < 4

    def step(v, carry):
        for i in range(8):
            a, b = src[2 * i, v], src[2 * i + 1, v]
            dst[2 * v, 8 * i : 8 * i + 8] = jnp.where(top, a, pltpu.roll(b, 4, 0))
            dst[2 * v + 1, 8 * i : 8 * i + 8] = jnp.where(top, pltpu.roll(a, 4, 0), b)
        return carry

    lax.fori_loop(0, 16, step, 0)


def kernel(
    target_hbm, source_hbm, right_hbm, forward_hbm, backward_hbm, middle_hbm, inverse_hbm,
    out_hbm,
    target_in, t, acc, s, wide, back, right, forward, backward, middle, inverse,
    send_sem, recv_sem, own_sem, table_sem, target_sem, out_sem,
):
    band, m = lax.axis_index("band"), lax.axis_index("member")
    bands = lax.axis_size("band")
    x, hi, core = m // 4, (m // 2) % 2, m % 2
    index = lambda x, hi, core: x * 4 + hi * 2 + core
    left, right_x, across = (x + 3) % 4, (x + 1) % 4, (x + 2) % 4
    to_sibling = {"member": index(x, hi, 1 - core)}
    to_z = {"member": index(x, 1 - hi, core)}
    to_left = {"member": index(left, hi, core)}
    to_right = {"member": index(right_x, hi, core)}
    to_next = {"band": (band + 1) % bands}
    to_prev = {"band": (band + bands - 1) % bands}

    barrier = pltpu.get_barrier_semaphore()
    for who in (to_z, to_left, to_right, to_next, to_prev, to_sibling):
        pl.semaphore_signal(barrier, inc=1, device_id=who, device_id_type=MESH)

    loads = [
        pltpu.make_async_copy(a, b, table_sem.at[i])
        for i, (a, b) in enumerate(
            ((right_hbm, right), (forward_hbm, forward), (backward_hbm, backward),
             (middle_hbm, middle), (inverse_hbm, inverse))
        )
    ]
    tiles = [
        pltpu.make_async_copy(target_hbm.at[0, :, pl.ds(128 * i, 128)], target_in.at[i], target_sem.at[i])
        for i in range(32)
    ]
    own = [pltpu.make_async_copy(source_hbm.at[k], s.at[k, m], own_sem.at[k]) for k in range(2)]
    for copy in (*own, *tiles, *loads):
        copy.start()

    started = []

    def send(k, slab, slot, who, src=None, unit=None):
        dst_unit = k if unit is None else unit
        copy = pltpu.make_async_remote_copy(
            src_ref=s.at[k, slab] if src is None else src,
            dst_ref=s.at[dst_unit, slab],
            send_sem=send_sem.at[k, slot],
            recv_sem=recv_sem.at[dst_unit, slab],
            device_id=who,
            device_id_type=MESH,
        )
        copy.start()
        started.append(copy)

    def arrived(k, slab):
        pltpu.make_async_remote_copy(
            src_ref=s.at[k, slab], dst_ref=s.at[k, slab],
            send_sem=send_sem.at[k, 0], recv_sem=recv_sem.at[k, slab],
            device_id=to_sibling, device_id_type=MESH,
        ).wait_recv()

    mz = index(x, 1 - hi, core)
    ml, mlz = index(left, hi, core), index(left, 1 - hi, core)
    mr, mrz = index(right_x, hi, core), index(right_x, 1 - hi, core)
    mo, moz = index(across, hi, core), index(across, 1 - hi, core)

    def stage_a(k):
        src = source_hbm.at[k] if k < 2 else None
        if k >= 2:
            arrived(k, m)
        send(k, m, 0, to_z, src)
        send(k, m, 1, to_left, src)
        send(k, m, 2, to_right, src)
        send(k, m, 3, to_sibling, src)

    def stage_b(k):
        arrived(k, mz)
        send(k, mz, 4, to_left)
        send(k, mz, 5, to_right)
        send(k, mz, 6, to_sibling)

    def stage_c(k):
        arrived(k, ml)
        send(k, ml, 7, to_right)
        send(k, ml, 8, to_sibling)
        arrived(k, mr)
        send(k, mr, 9, to_sibling)

    def stage_d(k):
        arrived(k, mrz)
        send(k, mrz, 10, to_left)
        send(k, mrz, 11, to_sibling)
        arrived(k, mlz)
        send(k, mlz, 12, to_sibling)

    def stage_e(k):
        arrived(k, mo)
        send(k, mo, 13, to_sibling)
        arrived(k, moz)
        send(k, moz, 14, to_sibling)

    def stage_f(k):
        for xx in range(4):
            for h in range(2):
                arrived(k, index(xx, h, 1 - core))
        if k < 2:
            own[k].wait()

    def first(k):
        lax.fori_loop(0, 8, lambda u, c: (forward_block(u, t, s.at[k], right, forward, wide), c)[1], 0, unroll=4)

    def second(k):
        lax.fori_loop(0, 4, lambda i, c: (middle_block(i // 2, i % 2, wide, middle, inverse, back), c)[1], 0, unroll=4)

    def third(k):
        lax.fori_loop(0, 8, lambda u, c: (backward_block(u, s.at[k], back, right, backward, acc, k == 0), c)[1], 0, unroll=4)

    pl.semaphore_wait(barrier, 6)
    stage_a(0)
    stage_a(1)
    for k in (2, 3):
        send(k, m, 15, to_next, source_hbm.at[k - 2])
    for copy in tiles:
        copy.wait()
    swap_in(target_in, t)
    for copy in loads:
        copy.wait()
    stage_b(0)
    stage_c(0)
    stage_a(2)
    stage_d(0)
    stage_b(1)
    stage_e(0)
    stage_c(1)
    stage_f(0)
    first(0)
    stage_d(1)
    stage_a(3)
    second(0)
    stage_b(2)
    stage_e(1)
    third(0)
    stage_c(2)
    stage_f(1)
    first(1)
    stage_d(2)
    second(1)
    stage_b(3)
    stage_e(2)
    third(1)
    stage_c(3)
    stage_f(2)
    first(2)
    stage_d(3)
    second(2)
    stage_e(3)
    third(2)
    stage_f(3)
    first(3)
    second(3)
    third(3)
    swap_out(acc, target_in)
    outs = [
        pltpu.make_async_copy(target_in.at[i], out_hbm.at[0, :, pl.ds(128 * i, 128)], out_sem.at[i])
        for i in range(32)
    ]
    for copy in outs:
        copy.start()
    for copy in started:
        copy.wait_send()
    for copy in outs:
        copy.wait()


def body(targets, sources):
    constants = [jnp.asarray(a) for a in tables()]
    slabs = sources.reshape(2, 4, 32, 128).transpose(0, 2, 1, 3).reshape(2, 16, 8, 128)
    anywhere = pl.BlockSpec(memory_space=pl.ANY)
    vmem, dma = pltpu.VMEM, pltpu.SemaphoreType.DMA
    return pl.pallas_call(
        kernel,
        out_shape=jax.ShapeDtypeStruct((1, 64, 4096), f32),
        in_specs=[anywhere] * 7,
        out_specs=anywhere,
        scratch_shapes=[
            vmem((32, 64, 128), f32), vmem((16, 16, 8, 128), f32), vmem((16, 16, 8, 128), f32),
            vmem((UNITS, 16, 16, 8, 128), f32),
            vmem((2, 2, 512, 256), bf16), vmem((2, 2, 256, 256), f32),
            *[vmem(a.shape, a.dtype) for a in constants],
            dma((UNITS, 16)), dma((UNITS, 16)), dma((2,)), dma((5,)), dma((32,)), dma((32,)),
        ],
        compiler_params=pltpu.CompilerParams(
            collective_id=0, has_side_effects=True, vmem_limit_bytes=56 * 2**20
        ),
        name="exchange",
    )(targets, slabs, *constants)


def solution(mesh):
    return jax.shard_map(
        body,
        mesh=mesh,
        in_specs=(P(("band", "member"), None, None), P("band", "member", None)),
        out_specs=P(("band", "member"), None, None),
        check_vma=False,
    )
```

profile of v0, /device:TPU:1, one launch (start us, length us, event | category | flops | bytes accessed | tf_op | source)
XLA Modules:
  0.0 57.6 jit_solution(16409930593205641171)
XLA Ops:
  0.0 55.3 %exchange.1 = f32[1,64,4096]{2,1,0:T(8,128)} custom-call(f32[1,64,4096]{2,1,0:T(8,128)} %target_hbm.1, f32[2,16,8,128]{3,2,1,0:T(8,128)} %bitcast.5, bf16[256,256]{1,0:T(8,128)(2,1)} %constant.10.clone.right_hbm, bf16[256,256]{1,0:T(8,128)(2,1)} %constant.11.clone.forward_hbm, bf16[256,256]{1,0:T(8,128)(2,1)} %constant.12.clone.backward_hbm, ...), custom_call_target="tpu_custom_call" | custom-call | tf_op jit(solution)/shard_map/exchange/pallas_call | solution.py:327
  55.3 2.3 %copy.10 = f32[1,64,4096]{2,1,0:T(8,128)} copy(f32[1,64,4096]{2,1,0:T(8,128)} %exchange.1) | data formatting | bytes 2097152
where the time goes:
time: 57.7 us; the launch traced here: 57.6 us
  Pallas kernels  55.3 us (96%)
  local copies, waits for them, and re-layouts  2.27 us (4%)
    pallas_call x1, Pallas kernels, body(): pl.pallas_call(kernel, out_shape=jax.ShapeDtypeStruct((1, 64, 4096), f32)...  55.3 us
    unnamed x1, local copies, waits for them, and re-layouts  2.27 us

commit v1 on v0

v1 whole, which is shorter than its diff:
```python
import numpy as np
import jax
import jax.numpy as jnp
from jax import lax
from jax.experimental import pallas as pl
from jax.experimental.pallas import tpu as pltpu
from jax.sharding import PartitionSpec as P

bf16 = jnp.bfloat16
f32 = jnp.float32
MESH = pl.DeviceIdType.MESH
UNITS = 4


def split_table(table):
    high = np.asarray(table, np.float32).astype(bf16)
    low = (table - high.astype(np.float64)).astype(np.float32).astype(bf16)
    return high, low


def tables():
    wave = np.arange(64) + 1.0
    sine = np.sin(np.pi * np.outer(wave, wave) / 65)
    single = 4 * np.sin(np.pi * wave / 130) ** 2
    high, low = split_table(np.kron(np.eye(2), sine))
    right = np.block([[high, low], [high, low]])
    plane = np.broadcast_to(np.arange(64).reshape(16, 1, 4), (16, 2, 4)).reshape(-1)
    block = np.broadcast_to(np.arange(2).reshape(1, 2, 1), (16, 2, 4)).reshape(-1)
    out_wave, out_block = np.tile(np.arange(64), 2), np.repeat(np.arange(2), 64)
    left = sine[out_wave][:, plane] * (out_block[:, None] == block[None, :])
    high, low = split_table(left)
    forward = np.block([[high, high], [low, low]])
    high, low = split_table(left.T)
    backward = np.block([[high, high], [low, low]])
    middle = []
    for parity in range(2):
        one = np.kron(sine[parity::2, :32], np.eye(8))
        for matrix in (one, one.T):
            high, low = split_table(matrix)
            middle.append(np.concatenate([high, low], axis=1))
    middle = np.stack(middle).reshape(2, 2, 256, 512)
    pair, low3, bit, top, k3 = np.meshgrid(*[np.arange(n) for n in (2, 8, 2, 2, 64)], indexing="ij")
    lanes = single[32 * top + 8 * (2 * pair + bit) + low3] + single[k3]
    lanes = lanes.reshape(2, 8, 256).astype(np.float32)
    rows = np.repeat(single[:, None], 256, axis=1).astype(np.float32)
    return right, forward, backward, middle, lanes, rows


def split(x):
    high = x.astype(bf16)
    return high, (x - high.astype(f32)).astype(bf16)


def dot(a, b):
    return jnp.dot(a, b, preferred_element_type=f32)


def exchange(a, b, low):
    return jnp.where(low, a, pltpu.roll(b, 64, 1)), jnp.where(low, pltpu.roll(a, 64, 1), b)


def forward_block(u, t, s, right, forward, wide):
    low = lax.broadcasted_iota(jnp.int32, (32, 128), 1) < 64
    d = jnp.concatenate([(t[:, v] * s[:, v]).reshape(128, 128) for v in (u, 15 - u)], axis=0)
    dh, dl = split(d)
    y = dot(jnp.concatenate([dh, dl], axis=1), right[...])
    y = y[:, :128] + y[:, 128:]
    w = [jnp.concatenate([q[:128], q[128:]], axis=1) for q in split(y)]
    z = dot(forward[...], jnp.concatenate(w, axis=0))
    z = z[:128] + z[128:]
    x = {}
    for side in range(2):
        lanes = slice(128 * side, 128 * side + 128)
        for l in range(2):
            a, b = z[64 * l : 64 * l + 32, lanes], z[64 * l + 32 : 64 * l + 64, lanes]
            x[side, l, 0], x[side, l, 1] = exchange(a, b, low)
    pairs = [(x[0, l, i], x[1, 1 - l, 1 - i]) for l in range(2) for i in range(2)]
    start = pl.multiple_of(u * 32, 32)
    for parity, parts in ((0, [a + b for a, b in pairs]), (1, [a - b for a, b in pairs])):
        for g in range(4):
            lanes = slice(128 * (g % 2), 128 * (g % 2) + 128)
            high, rest = split(jnp.concatenate([q[8 * g : 8 * g + 8] for q in parts], axis=0))
            wide[parity, g // 2, pl.ds(start, 32), lanes] = high
            wide[parity, g // 2, pl.ds(256 + start, 32), lanes] = rest


def middle_block(parity, pair, wide, middle, inverse, back):
    def times(way, high, low):
        w = middle[parity, way]
        sides = jnp.concatenate([w[:, :256], w], axis=1)
        return dot(sides, jnp.concatenate([high, low, high], axis=0))

    e = wide[parity, pair]
    q = times(0, e[:256], e[256:]) * inverse[parity, pair]
    back[parity, pair] = times(1, *split(q))


def backward_block(u, s, back, right, backward, out, first, emit=None):
    low = lax.broadcasted_iota(jnp.int32, (32, 128), 1) < 64
    start = pl.multiple_of(u * 32, 32)
    total, differ = [[] for _ in range(4)], [[] for _ in range(4)]
    for g in range(4):
        lanes = slice(128 * (g % 2), 128 * (g % 2) + 128)
        even, odd = (back[p, g // 2, pl.ds(start, 32), lanes] for p in range(2))
        plus, minus = even + odd, even - odd
        for a in range(4):
            total[a].append(plus[8 * a : 8 * a + 8])
            differ[a].append(minus[8 * a : 8 * a + 8])
    total = [jnp.concatenate(q, axis=0) for q in total]
    differ = [jnp.concatenate(q, axis=0) for q in differ][::-1]
    z = []
    for side in (total, differ):
        z.append(jnp.concatenate([*exchange(side[0], side[1], low), *exchange(side[2], side[3], low)], axis=0))
    y = dot(backward[...], jnp.concatenate(split(jnp.concatenate(z, axis=1)), axis=0))
    y = y[:128] + y[128:]
    y = jnp.concatenate([y[:, :128], y[:, 128:]], axis=0)
    q = dot(jnp.concatenate(split(y), axis=1), right[...])
    q = q[:, :128] + q[:, 128:]
    for side, v in ((0, u), (1, 15 - u)):
        term = s[:, v] * q[128 * side : 128 * side + 128].reshape(16, 8, 128)
        if emit is None:
            out[:, v] = -term if first else out[:, v] - term
        else:
            emit(v, out[:, v] - term)


def swap_in(src, dst):
    top = lax.broadcasted_iota(jnp.int32, (8, 128), 0) < 4

    def step(v, carry):
        for i in range(8):
            a, b = src[2 * v, 8 * i : 8 * i + 8], src[2 * v + 1, 8 * i : 8 * i + 8]
            dst[2 * i, v] = jnp.where(top, a, pltpu.roll(b, 4, 0))
            dst[2 * i + 1, v] = jnp.where(top, pltpu.roll(a, 4, 0), b)
        return carry

    lax.fori_loop(0, 16, step, 0)


def swapped(value):
    top = lax.broadcasted_iota(jnp.int32, (8, 8, 128), 1) < 4
    value = value.reshape(8, 2, 8, 128)
    a, b = value[:, 0], value[:, 1]
    one, two = jnp.where(top, a, pltpu.roll(b, 4, 1)), jnp.where(top, pltpu.roll(a, 4, 1), b)
    return one.reshape(64, 128), two.reshape(64, 128)


def fill_inverse(lanes, rows, inverse):
    factor = (2.0 / 65) ** 3

    def step(m, carry):
        start = pl.multiple_of(8 * m, 8)
        for parity in range(2):
            for pair in range(2):
                eigen = lanes[pair] + rows[pl.ds(2 * m + parity, 1), :]
                inverse[parity, pair, pl.ds(start, 8), :] = factor / eigen
        return carry

    lax.fori_loop(0, 32, step, 0)


def kernel(
    target_hbm, source_hbm, right_hbm, forward_hbm, backward_hbm, middle_hbm, lanes_hbm, rows_hbm,
    out_hbm,
    tiles, t, acc, s, wide, back, inverse, right, forward, backward, middle, lanes, rows,
    link_sem, pass_sem, recv_sem, sibling_sem, own_sem, table_sem, target_sem, out_sem,
):
    band, m = lax.axis_index("band"), lax.axis_index("member")
    bands = lax.axis_size("band")
    columns = bands // 4
    row, column = band // columns, band % columns
    x, hi, core = m // 4, (m // 2) % 2, m % 2
    index = lambda x, hi, core: x * 4 + hi * 2 + core
    left, right_x, across = (x + 3) % 4, (x + 1) % 4, (x + 2) % 4
    to_flip = jnp.where((row == 3) & (column == columns - 1), 1, 0)
    from_flip = jnp.where((row == 0) & (column == 0), 1, 0)
    near = (hi + from_flip) % 2
    to_sibling = {"member": index(x, hi, 1 - core)}
    to_z = {"member": index(x, 1 - hi, core)}
    to_left, to_right = ({"member": index(xx, hi, core)} for xx in (left, right_x))
    to_next = {"band": (band + 1) % bands, "member": index(x, (hi + to_flip) % 2, core)}
    to_prev = {"band": (band + bands - 1) % bands, "member": index(x, near, core)}

    barrier = pltpu.get_barrier_semaphore()
    for who in (to_z, to_left, to_right, to_next, to_prev, to_sibling):
        pl.semaphore_signal(barrier, inc=1, device_id=who, device_id_type=MESH)

    loads = [
        pltpu.make_async_copy(a, b, table_sem.at[i])
        for i, (a, b) in enumerate(
            ((right_hbm, right), (forward_hbm, forward), (backward_hbm, backward),
             (middle_hbm, middle), (lanes_hbm, lanes), (rows_hbm, rows))
        )
    ]
    own = [pltpu.make_async_copy(source_hbm.at[k], s.at[k, m], own_sem.at[k]) for k in range(2)]
    for copy in (*own, *loads):
        copy.start()
    for i in range(32):
        pltpu.make_async_copy(target_hbm.at[0, :, pl.ds(128 * i, 128)], tiles.at[i], target_sem).start()

    def remote(k, slab, piece, who, src, unit):
        window = pl.ds(8 * piece, 8)
        return pltpu.make_async_remote_copy(
            src_ref=s.at[unit, slab, window] if src is None else src.at[window],
            dst_ref=s.at[k, slab, window],
            send_sem=link_sem.at[unit],
            recv_sem=recv_sem.at[k, slab, piece],
            device_id=who,
            device_id_type=MESH,
        )

    def send(k, slab, piece, who, src=None, unit=None):
        remote(k, slab, piece, who, src, k if unit is None else unit).start()

    def arrived(k, slab, piece):
        remote(k, slab, piece, to_left, None, k).wait_recv()

    def share(k, slab, src=None):
        pltpu.make_async_remote_copy(
            src_ref=s.at[k, slab] if src is None else src,
            dst_ref=s.at[k, slab],
            send_sem=pass_sem.at[k],
            recv_sem=sibling_sem.at[k],
            device_id=to_sibling,
            device_id_type=MESH,
        ).start()

    def group(k, count, send_sem, recv_sem):
        block = s.at[k, pl.ds(0, count)]
        return pltpu.make_async_remote_copy(
            src_ref=block, dst_ref=block, send_sem=send_sem, recv_sem=recv_sem,
            device_id=to_sibling, device_id_type=MESH,
        )

    mine, other = index(x, hi, core), index(x, 1 - hi, core)
    halves = range(2)

    def other_out(k):
        for piece in halves:
            arrived(k, other, piece)
            for who in (to_left, to_right):
                send(k, other, piece, who)
        for piece in halves:
            send(k + 2, other, piece, to_next, unit=k)
        share(k, other)

    def passed_out(k, half):
        slab = index(x, half, core)
        for piece in halves:
            arrived(k, slab, piece)
            for who in (to_left, to_right):
                send(k, slab, piece, who)
        share(k, slab)

    def sides(k, half, onward):
        from_left, from_right = index(left, half, core), index(right_x, half, core)
        arrived(k, from_left, 0)
        if onward:
            send(k, from_left, 0, to_right)
        arrived(k, from_left, 1)
        arrived(k, from_right, 0)
        arrived(k, from_right, 1)
        if onward:
            send(k, from_right, 1, to_left)
        share(k, from_left)
        share(k, from_right)

    def far(k, half, onward):
        slab = index(across, half, core)
        for piece in halves:
            arrived(k, slab, piece)
            if onward:
                send(k + 2, slab, piece, to_next, unit=k)
        share(k, slab)

    def complete(k):
        group(k, 8, pass_sem.at[k], sibling_sem.at[k]).wait_recv()

    def first(k):
        for u in range(8):
            forward_block(u, t, s.at[k], right, forward, wide)

    def second(k):
        for i in range(4):
            middle_block(i // 2, i % 2, wide, middle, inverse, back)

    def third(k, emit=None):
        for u in range(8):
            backward_block(u, s.at[k], back, right, backward, acc, k == 0, emit)

    def emit(v, value):
        for i, tile in enumerate(swapped(value)):
            tiles[2 * v + i] = tile
            where = out_hbm.at[0, :, pl.ds(128 * (2 * v + i), 128)]
            pltpu.make_async_copy(tiles.at[2 * v + i], where, out_sem).start()

    pl.semaphore_wait(barrier, 6)
    for k in range(2):
        for piece in halves:
            send(k, mine, piece, to_z, source_hbm.at[k])
        for piece in halves:
            for who in (to_left, to_right):
                send(k, mine, piece, who, source_hbm.at[k])
        for piece in halves:
            send(k + 2, mine, piece, to_next, source_hbm.at[k], unit=k)
    for k in range(2):
        share(k, mine, source_hbm.at[k])
    pltpu.make_async_copy(tiles, tiles, target_sem).wait()
    swap_in(tiles, t)
    for copy in (*loads, *own):
        copy.wait()
    fill_inverse(lanes, rows, inverse)
    sides(0, hi, True)
    passed_out(2, near)
    sides(1, hi, True)
    passed_out(3, near)
    far(0, hi, True)
    other_out(0)
    sides(2, near, False)
    far(1, hi, True)
    sides(3, near, False)
    other_out(1)
    sides(0, 1 - hi, True)
    passed_out(2, 1 - near)
    far(0, 1 - hi, True)
    complete(0)
    first(0)
    sides(1, 1 - hi, True)
    passed_out(3, 1 - near)
    second(0)
    far(1, 1 - hi, True)
    sides(2, 1 - near, False)
    third(0)
    far(2, near, False)
    far(2, 1 - near, False)
    complete(1)
    first(1)
    sides(3, 1 - near, False)
    far(3, near, False)
    second(1)
    third(1)
    far(3, 1 - near, False)
    complete(2)
    first(2)
    second(2)
    third(2)
    complete(3)
    first(3)
    for k in range(UNITS):
        group(k, 8, pass_sem.at[k], sibling_sem.at[k]).wait_send()
        group(k, 11 if k < 2 else 4, link_sem.at[k], sibling_sem.at[k]).wait_send()
    second(3)
    third(3, emit)
    pltpu.make_async_copy(tiles, tiles, out_sem).wait()


def body(targets, sources):
    constants = [jnp.asarray(a) for a in tables()]
    slabs = sources.reshape(2, 4, 32, 128).transpose(0, 2, 1, 3).reshape(2, 16, 8, 128)
    anywhere = pl.BlockSpec(memory_space=pl.ANY)
    vmem, dma = pltpu.VMEM, pltpu.SemaphoreType.DMA
    return pl.pallas_call(
        kernel,
        out_shape=jax.ShapeDtypeStruct((1, 64, 4096), f32),
        in_specs=[anywhere] * 8,
        out_specs=anywhere,
        scratch_shapes=[
            vmem((32, 64, 128), f32), vmem((16, 16, 8, 128), f32), vmem((16, 16, 8, 128), f32),
            vmem((UNITS, 16, 16, 8, 128), f32),
            vmem((2, 2, 512, 256), bf16), vmem((2, 2, 256, 256), f32), vmem((2, 2, 256, 256), f32),
            *[vmem(a.shape, a.dtype) for a in constants],
            dma((UNITS,)), dma((UNITS,)), dma((UNITS, 16, 2)), dma((UNITS,)),
            dma((2,)), dma((6,)), dma, dma,
        ],
        compiler_params=pltpu.CompilerParams(
            collective_id=0, has_side_effects=True, vmem_limit_bytes=56 * 2**20
        ),
        name="exchange",
    )(targets, slabs, *constants)


def solution(mesh):
    return jax.shard_map(
        body,
        mesh=mesh,
        in_specs=(P(("band", "member"), None, None), P("band", "member", None)),
        out_specs=P(("band", "member"), None, None),
        check_vma=False,
    )
```

time: 57.7 us -> 54.5 us (0.945)
  Pallas kernels: 55.3 us -> 52 us
    pallas_call x1, Pallas kernels: 55.3 us -> 52 us  [body(): pl.pallas_call(kernel, out_shape=jax.ShapeDtypeStruct((1, 64, 4096), f32)...]
where the time goes in v1:
time: 54.5 us; the launch traced here: 54.3 us
  Pallas kernels  52 us (95%)
  local copies, waits for them, and re-layouts  2.27 us (4%)
    pallas_call x1, Pallas kernels, body(): pl.pallas_call(kernel, out_shape=jax.ShapeDtypeStruct((1, 64, 4096), f32)...  52 us
    unnamed x1, local copies, waits for them, and re-layouts  2.27 us

profile of v1, /device:TPU:1, one launch (start us, length us, event | category | flops | bytes accessed | tf_op | source)
XLA Modules:
  0.0 54.3 jit_solution(6862582150928862642)
XLA Ops:
  0.0 52.0 %exchange.1 = f32[1,64,4096]{2,1,0:T(8,128)} custom-call(f32[1,64,4096]{2,1,0:T(8,128)} %target_hbm.1, f32[2,16,8,128]{3,2,1,0:T(8,128)} %bitcast.5, bf16[256,256]{1,0:T(8,128)(2,1)} %constant.12.clone.right_hbm, bf16[256,256]{1,0:T(8,128)(2,1)} %constant.13.clone.forward_hbm, bf16[256,256]{1,0:T(8,128)(2,1)} %constant.14.clone.backward_hbm, ...), custom_call_target="tpu_custom_call" | custom-call | tf_op jit(solution)/shard_map/exchange/pallas_call | solution.py:362
  52.0 2.3 %copy.11 = f32[1,64,4096]{2,1,0:T(8,128)} copy(f32[1,64,4096]{2,1,0:T(8,128)} %exchange.1) | data formatting | bytes 2097152

commit v2 on v1

--- a/solution.py
+++ b/solution.py
@@ -9,6 +9,7 @@
 bf16 = jnp.bfloat16
 f32 = jnp.float32
 MESH = pl.DeviceIdType.MESH
+ROWS = 8
 UNITS = 4
 
 
@@ -168,18 +169,17 @@
     band, m = lax.axis_index("band"), lax.axis_index("member")
     bands = lax.axis_size("band")
     columns = bands // 4
-    row, column = band // columns, band % columns
+    column = band % columns
     x, hi, core = m // 4, (m // 2) % 2, m % 2
     index = lambda x, hi, core: x * 4 + hi * 2 + core
     left, right_x, across = (x + 3) % 4, (x + 1) % 4, (x + 2) % 4
-    to_flip = jnp.where((row == 3) & (column == columns - 1), 1, 0)
-    from_flip = jnp.where((row == 0) & (column == 0), 1, 0)
-    near = (hi + from_flip) % 2
+    to_wrap = jnp.where(column == columns - 1, 1, 0)
+    from_wrap = jnp.where(column == 0, 1, 0)
     to_sibling = {"member": index(x, hi, 1 - core)}
     to_z = {"member": index(x, 1 - hi, core)}
     to_left, to_right = ({"member": index(xx, hi, core)} for xx in (left, right_x))
-    to_next = {"band": (band + 1) % bands, "member": index(x, (hi + to_flip) % 2, core)}
-    to_prev = {"band": (band + bands - 1) % bands, "member": index(x, near, core)}
+    to_next = {"band": (band + 1) % bands}
+    to_prev = {"band": (band + bands - 1) % bands}
 
     barrier = pltpu.get_barrier_semaphore()
     for who in (to_z, to_left, to_right, to_next, to_prev, to_sibling):
@@ -199,7 +199,7 @@
         pltpu.make_async_copy(target_hbm.at[0, :, pl.ds(128 * i, 128)], tiles.at[i], target_sem).start()
 
     def remote(k, slab, piece, who, src, unit):
-        window = pl.ds(8 * piece, 8)
+        window = pl.ds(ROWS * piece, ROWS)
         return pltpu.make_async_remote_copy(
             src_ref=s.at[unit, slab, window] if src is None else src.at[window],
             dst_ref=s.at[k, slab, window],
@@ -233,45 +233,78 @@
         )
 
     mine, other = index(x, hi, core), index(x, 1 - hi, core)
-    halves = range(2)
-
-    def other_out(k):
-        for piece in halves:
+    pieces = range(16 // ROWS)
+
+    def own_next():
+        for k in range(2):
+            for piece in pieces:
+                send(k + 2, mine, piece, to_next, source_hbm.at[k], unit=k)
+
+    def passed(wrap, *which):
+        @pl.when(from_wrap == wrap)
+        def _():
+            for k, half in which:
+                passed_out(k, half)
+
+    def other_out(k, some=pieces):
+        for piece in some:
             arrived(k, other, piece)
             for who in (to_left, to_right):
                 send(k, other, piece, who)
-        for piece in halves:
             send(k + 2, other, piece, to_next, unit=k)
-        share(k, other)
+        if pieces[-1] in some:
+            share(k, other)
 
     def passed_out(k, half):
         slab = index(x, half, core)
-        for piece in halves:
+        for piece in pieces:
             arrived(k, slab, piece)
             for who in (to_left, to_right):
                 send(k, slab, piece, who)
         share(k, slab)
 
-    def sides(k, half, onward):
+    def sides(k, half):
         from_left, from_right = index(left, half, core), index(right_x, half, core)
-        arrived(k, from_left, 0)
-        if onward:
-            send(k, from_left, 0, to_right)
-        arrived(k, from_left, 1)
-        arrived(k, from_right, 0)
-        arrived(k, from_right, 1)
-        if onward:
-            send(k, from_right, 1, to_left)
+
+        def relay(piece):
+            if piece < len(pieces) // 2:
+                send(k, from_left, piece, to_right)
+            else:
+                send(k, from_right, piece, to_left)
+
+        for piece in pieces:
+            arrived(k, from_left, piece)
+            arrived(k, from_right, piece)
+            if k < 2:
+                relay(piece)
+        if k >= 2:
+            @pl.when(from_wrap == 1)
+            def _():
+                for piece in pieces:
+                    relay(piece)
+
         share(k, from_left)
         share(k, from_right)
 
-    def far(k, half, onward):
+    def far(k, half):
         slab = index(across, half, core)
-        for piece in halves:
+        for piece in pieces:
             arrived(k, slab, piece)
-            if onward:
-                send(k + 2, slab, piece, to_next, unit=k)
+        if k < 2:
+            @pl.when(to_wrap == 0)
+            def _():
+                for piece in pieces:
+                    send(k + 2, slab, piece, to_next, unit=k)
+
         share(k, slab)
+
+    def sent(k):
+        group(k, 8, pass_sem.at[k], sibling_sem.at[k]).wait_send()
+        flag = to_wrap if k < 2 else from_wrap
+        for value, count in ((0, 11 if k < 2 else 4), (1, 9 if k < 2 else 6)):
+            @pl.when(flag == value)
+            def _():
+                group(k, count, link_sem.at[k], sibling_sem.at[k]).wait_send()
 
     def complete(k):
         group(k, 8, pass_sem.at[k], sibling_sem.at[k]).wait_recv()
@@ -296,13 +329,13 @@
 
     pl.semaphore_wait(barrier, 6)
     for k in range(2):
-        for piece in halves:
+        for piece in pieces:
             send(k, mine, piece, to_z, source_hbm.at[k])
-        for piece in halves:
+        for piece in pieces:
             for who in (to_left, to_right):
                 send(k, mine, piece, who, source_hbm.at[k])
-        for piece in halves:
-            send(k + 2, mine, piece, to_next, source_hbm.at[k], unit=k)
+        if k == 0:
+            pl.when(to_wrap == 0)(own_next)
     for k in range(2):
         share(k, mine, source_hbm.at[k])
     pltpu.make_async_copy(tiles, tiles, target_sem).wait()
@@ -310,36 +343,40 @@
     for copy in (*loads, *own):
         copy.wait()
     fill_inverse(lanes, rows, inverse)
-    sides(0, hi, True)
-    passed_out(2, near)
-    sides(1, hi, True)
-    passed_out(3, near)
-    far(0, hi, True)
+    sides(0, hi)
+    sides(1, hi)
+    passed(0, (2, hi))
+    pl.when(to_wrap == 1)(own_next)
     other_out(0)
-    sides(2, near, False)
-    far(1, hi, True)
-    sides(3, near, False)
+    far(0, hi)
+    passed(0, (3, hi))
     other_out(1)
-    sides(0, 1 - hi, True)
-    passed_out(2, 1 - near)
-    far(0, 1 - hi, True)
+    sides(0, 1 - hi)
+    passed(1, (2, hi))
+    far(1, hi)
+    passed(0, (2, 1 - hi))
+    far(0, 1 - hi)
+    passed(1, (3, hi))
+    sides(1, 1 - hi)
     complete(0)
     first(0)
-    sides(1, 1 - hi, True)
-    passed_out(3, 1 - near)
+    passed(0, (3, 1 - hi))
+    passed(1, (2, 1 - hi), (3, 1 - hi))
+    sides(2, hi)
     second(0)
-    far(1, 1 - hi, True)
-    sides(2, 1 - near, False)
+    far(1, 1 - hi)
+    sides(3, hi)
     third(0)
-    far(2, near, False)
-    far(2, 1 - near, False)
+    sides(2, 1 - hi)
     complete(1)
     first(1)
-    sides(3, 1 - near, False)
-    far(3, near, False)
+    far(2, hi)
+    sides(3, 1 - hi)
     second(1)
+    far(2, 1 - hi)
     third(1)
-    far(3, 1 - near, False)
+    far(3, hi)
+    far(3, 1 - hi)
     complete(2)
     first(2)
     second(2)
@@ -347,8 +384,7 @@
     complete(3)
     first(3)
     for k in range(UNITS):
-        group(k, 8, pass_sem.at[k], sibling_sem.at[k]).wait_send()
-        group(k, 11 if k < 2 else 4, link_sem.at[k], sibling_sem.at[k]).wait_send()
+        sent(k)
     second(3)
     third(3, emit)
     pltpu.make_async_copy(tiles, tiles, out_sem).wait()
@@ -369,7 +405,7 @@
             vmem((UNITS, 16, 16, 8, 128), f32),
             vmem((2, 2, 512, 256), bf16), vmem((2, 2, 256, 256), f32), vmem((2, 2, 256, 256), f32),
             *[vmem(a.shape, a.dtype) for a in constants],
-            dma((UNITS,)), dma((UNITS,)), dma((UNITS, 16, 2)), dma((UNITS,)),
+            dma((UNITS,)), dma((UNITS,)), dma((UNITS, 16, 16 // ROWS)), dma((UNITS,)),
             dma((2,)), dma((6,)), dma, dma,
         ],
         compiler_params=pltpu.CompilerParams(

time: 54.5 us -> 55.5 us (1.018)
  Pallas kernels: 52 us -> 53.1 us
    pallas_call x1, Pallas kernels: 52 us -> 53.1 us  [body(): pl.pallas_call(kernel, out_shape=jax.ShapeDtypeStruct((1, 64, 4096), f32)...]
where the time goes in v2:
time: 55.5 us; the launch traced here: 55.4 us
  Pallas kernels  53.1 us (96%)
  local copies, waits for them, and re-layouts  2.27 us (4%)
    pallas_call x1, Pallas kernels, body(): pl.pallas_call(kernel, out_shape=jax.ShapeDtypeStruct((1, 64, 4096), f32)...  53.1 us
    unnamed x1, local copies, waits for them, and re-layouts  2.27 us

profile of v2, /device:TPU:1, one launch (start us, length us, event | category | flops | bytes accessed | tf_op | source)
XLA Modules:
  0.0 55.4 jit_solution(942444968244397534)
XLA Ops:
  0.0 53.1 %exchange.1 = f32[1,64,4096]{2,1,0:T(8,128)} custom-call(f32[1,64,4096]{2,1,0:T(8,128)} %target_hbm.1, f32[2,16,8,128]{3,2,1,0:T(8,128)} %bitcast.5, bf16[256,256]{1,0:T(8,128)(2,1)} %constant.12.clone.right_hbm, bf16[256,256]{1,0:T(8,128)(2,1)} %constant.13.clone.forward_hbm, bf16[256,256]{1,0:T(8,128)(2,1)} %constant.14.clone.backward_hbm, ...), custom_call_target="tpu_custom_call" | custom-call | tf_op jit(solution)/shard_map/exchange/pallas_call | solution.py:398
  53.1 2.3 %copy.11 = f32[1,64,4096]{2,1,0:T(8,128)} copy(f32[1,64,4096]{2,1,0:T(8,128)} %exchange.1) | data formatting | bytes 2097152

commit v3 on v2

--- a/solution.py
+++ b/solution.py
@@ -235,17 +235,6 @@
     mine, other = index(x, hi, core), index(x, 1 - hi, core)
     pieces = range(16 // ROWS)
 
-    def own_next():
-        for k in range(2):
-            for piece in pieces:
-                send(k + 2, mine, piece, to_next, source_hbm.at[k], unit=k)
-
-    def passed(wrap, *which):
-        @pl.when(from_wrap == wrap)
-        def _():
-            for k, half in which:
-                passed_out(k, half)
-
     def other_out(k, some=pieces):
         for piece in some:
             arrived(k, other, piece)
@@ -334,8 +323,8 @@
         for piece in pieces:
             for who in (to_left, to_right):
                 send(k, mine, piece, who, source_hbm.at[k])
-        if k == 0:
-            pl.when(to_wrap == 0)(own_next)
+        for piece in pieces:
+            send(k + 2, mine, piece, to_next, source_hbm.at[k], unit=k)
     for k in range(2):
         share(k, mine, source_hbm.at[k])
     pltpu.make_async_copy(tiles, tiles, target_sem).wait()
@@ -345,38 +334,34 @@
     fill_inverse(lanes, rows, inverse)
     sides(0, hi)
     sides(1, hi)
-    passed(0, (2, hi))
-    pl.when(to_wrap == 1)(own_next)
+    passed_out(2, hi)
     other_out(0)
     far(0, hi)
-    passed(0, (3, hi))
+    passed_out(3, hi)
+    sides(0, 1 - hi)
+    far(1, hi)
+    sides(2, hi)
     other_out(1)
-    sides(0, 1 - hi)
-    passed(1, (2, hi))
-    far(1, hi)
-    passed(0, (2, 1 - hi))
+    sides(3, hi)
     far(0, 1 - hi)
-    passed(1, (3, hi))
-    sides(1, 1 - hi)
+    passed_out(2, 1 - hi)
     complete(0)
     first(0)
-    passed(0, (3, 1 - hi))
-    passed(1, (2, 1 - hi), (3, 1 - hi))
-    sides(2, hi)
+    sides(1, 1 - hi)
+    passed_out(3, 1 - hi)
+    sides(2, 1 - hi)
     second(0)
     far(1, 1 - hi)
-    sides(3, hi)
     third(0)
-    sides(2, 1 - hi)
+    far(2, hi)
+    sides(3, 1 - hi)
     complete(1)
     first(1)
-    far(2, hi)
-    sides(3, 1 - hi)
+    far(2, 1 - hi)
+    far(3, hi)
     second(1)
-    far(2, 1 - hi)
+    far(3, 1 - hi)
     third(1)
-    far(3, hi)
-    far(3, 1 - hi)
     complete(2)
     first(2)
     second(2)

time: 55.5 us -> 50.9 us (0.917)
  Pallas kernels: 53.1 us -> 48.5 us
    pallas_call x1, Pallas kernels: 53.1 us -> 48.5 us  [body(): pl.pallas_call(kernel, out_shape=jax.ShapeDtypeStruct((1, 64, 4096), f32)...]
where the time goes in v3:
time: 50.9 us; the launch traced here: 50.7 us
  Pallas kernels  48.5 us (95%)
  local copies, waits for them, and re-layouts  2.27 us (4%)
    pallas_call x1, Pallas kernels, body(): pl.pallas_call(kernel, out_shape=jax.ShapeDtypeStruct((1, 64, 4096), f32)...  48.5 us
    unnamed x1, local copies, waits for them, and re-layouts  2.27 us

profile of v3, /device:TPU:1, one launch (start us, length us, event | category | flops | bytes accessed | tf_op | source)
XLA Modules:
  0.0 50.7 jit_solution(9993565745415878219)
XLA Ops:
  0.0 48.5 %exchange.1 = f32[1,64,4096]{2,1,0:T(8,128)} custom-call(f32[1,64,4096]{2,1,0:T(8,128)} %target_hbm.1, f32[2,16,8,128]{3,2,1,0:T(8,128)} %bitcast.5, bf16[256,256]{1,0:T(8,128)(2,1)} %constant.12.clone.right_hbm, bf16[256,256]{1,0:T(8,128)(2,1)} %constant.13.clone.forward_hbm, bf16[256,256]{1,0:T(8,128)(2,1)} %constant.14.clone.backward_hbm, ...), custom_call_target="tpu_custom_call" | custom-call | tf_op jit(solution)/shard_map/exchange/pallas_call | solution.py:383
  48.5 2.3 %copy.11 = f32[1,64,4096]{2,1,0:T(8,128)} copy(f32[1,64,4096]{2,1,0:T(8,128)} %exchange.1) | data formatting | bytes 2097152

commit v4 on v3

--- a/solution.py
+++ b/solution.py
@@ -162,9 +162,9 @@
 
 def kernel(
     target_hbm, source_hbm, right_hbm, forward_hbm, backward_hbm, middle_hbm, lanes_hbm, rows_hbm,
-    out_hbm,
+    out,
     tiles, t, acc, s, wide, back, inverse, right, forward, backward, middle, lanes, rows,
-    link_sem, pass_sem, recv_sem, sibling_sem, own_sem, table_sem, target_sem, out_sem,
+    link_sem, pass_sem, recv_sem, sibling_sem, own_sem, table_sem, target_sem,
 ):
     band, m = lax.axis_index("band"), lax.axis_index("member")
     bands = lax.axis_size("band")
@@ -312,9 +312,7 @@
 
     def emit(v, value):
         for i, tile in enumerate(swapped(value)):
-            tiles[2 * v + i] = tile
-            where = out_hbm.at[0, :, pl.ds(128 * (2 * v + i), 128)]
-            pltpu.make_async_copy(tiles.at[2 * v + i], where, out_sem).start()
+            out[0, :, 128 * (2 * v + i) : 128 * (2 * v + i) + 128] = tile
 
     pl.semaphore_wait(barrier, 6)
     for k in range(2):
@@ -372,7 +370,6 @@
         sent(k)
     second(3)
     third(3, emit)
-    pltpu.make_async_copy(tiles, tiles, out_sem).wait()
 
 
 def body(targets, sources):
@@ -382,19 +379,19 @@
     vmem, dma = pltpu.VMEM, pltpu.SemaphoreType.DMA
     return pl.pallas_call(
         kernel,
-        out_shape=jax.ShapeDtypeStruct((1, 64, 4096), f32),
+        out_shape=vmem((1, 64, 4096), f32),
         in_specs=[anywhere] * 8,
-        out_specs=anywhere,
+        out_specs=pl.BlockSpec(memory_space=vmem),
         scratch_shapes=[
             vmem((32, 64, 128), f32), vmem((16, 16, 8, 128), f32), vmem((16, 16, 8, 128), f32),
             vmem((UNITS, 16, 16, 8, 128), f32),
             vmem((2, 2, 512, 256), bf16), vmem((2, 2, 256, 256), f32), vmem((2, 2, 256, 256), f32),
             *[vmem(a.shape, a.dtype) for a in constants],
             dma((UNITS,)), dma((UNITS,)), dma((UNITS, 16, 16 // ROWS)), dma((UNITS,)),
-            dma((2,)), dma((6,)), dma, dma,
+            dma((2,)), dma((6,)), dma,
         ],
         compiler_params=pltpu.CompilerParams(
-            collective_id=0, has_side_effects=True, vmem_limit_bytes=56 * 2**20
+            collective_id=0, has_side_effects=True, vmem_limit_bytes=65900000
         ),
         name="exchange",
     )(targets, slabs, *constants)

time: 50.9 us -> 48.9 us (0.961)
  local copies, waits for them, and re-layouts: 2.27 us -> 0.97 us
  Pallas kernels: 48.5 us -> 47.8 us
    unnamed x1, local copies, waits for them, and re-layouts: 2.27 us -> 0.97 us
    pallas_call x1, Pallas kernels: 48.5 us -> 47.8 us  [body(): pl.pallas_call(kernel, out_shape=vmem((1, 64, 4096), f32), in_specs=[anyw...]
where the time goes in v4:
time: 48.9 us; the launch traced here: 48.8 us
  Pallas kernels  47.8 us (98%)
  local copies, waits for them, and re-layouts  0.97 us (2%)
    pallas_call x1, Pallas kernels, body(): pl.pallas_call(kernel, out_shape=vmem((1, 64, 4096), f32), in_specs=[anyw...  47.8 us

profile of v4, /device:TPU:1, one launch (start us, length us, event | category | flops | bytes accessed | tf_op | source)
XLA Modules:
  0.0 48.8 jit_solution(8251884478100987506)
XLA Ops:
  0.0 47.8 %exchange.1 = f32[1,64,4096]{2,1,0:T(8,128)S(1)} custom-call(f32[1,64,4096]{2,1,0:T(8,128)} %target_hbm.1, f32[2,16,8,128]{3,2,1,0:T(8,128)} %bitcast.5, bf16[256,256]{1,0:T(8,128)(2,1)} %constant.12.clone.right_hbm, bf16[256,256]{1,0:T(8,128)(2,1)} %constant.13.clone.forward_hbm, bf16[256,256]{1,0:T(8,128)(2,1)} %constant.14.clone.backward_hbm, ...), custom_call_target="tpu_custom_call" | custom-call | tf_op jit(solution)/shard_map/exchange/pallas_call | solution.py:380
  47.8 1.0 %copy.11 = f32[1,64,4096]{2,1,0:T(8,128)} copy(f32[1,64,4096]{2,1,0:T(8,128)S(1)} %exchange.1) | data formatting | bytes 2097152
